TPU v7x, 32 devices: a whole 2x2x4 slice. The times are simulated.
32 devices in a mesh: grid: 8 (over y, x, core), orb: 4 (over z).
Axes of the slice: x: 2, y: 2, z: 4, core: 2. Of those that a mesh axis runs over, the one named last changes fastest.
Arguments:
- orbitals: float32 [512, 32, 8, 128], P('orb', 'grid'), may hold values from -13 to 13, as said below
- potential: float32 [32, 8, 128], P('grid'), may hold values from -1 to 1
Outputs:
- orthonormal: float32 [512, 32, 8, 128], P('orb', 'grid')
Inputs may be any that keep to these rules, and one draw needn't show every extreme that they name: Trial orbitals, real-valued.
All inputs are finite; a program needn't handle non-finite values.
Results may differ from a plain program's by a relative error of at most 0.0003.
Values sent between devices are 32-bit elements; how exact they have to be, the bound alone decides.
No kernel may reach another device: no remote copies, remote signals or barrier semaphores. Data moves between devices by JAX's collectives and lax.ppermute only.
A program may use at most 64 MiB of HBM per device.

v0:
```python
import jax
import jax.numpy as jnp
from jax import lax
from jax.sharding import PartitionSpec as P

lap_weights = (-205.0 / 72.0, 8.0 / 5.0, -1.0 / 5.0, 8.0 / 315.0, -1.0 / 560.0)
lower_edge = 3.0
upper_edge = 11.0


def wrap_pad(field, axis_num):
    length = field.shape[axis_num]
    head = lax.slice_in_dim(field, length - 4, length, axis=axis_num)
    tail = lax.slice_in_dim(field, 0, 4, axis=axis_num)
    return jnp.concatenate([head, field, tail], axis=axis_num)


def operate(padded_x, field, potential):
    planes = field.shape[1]
    rows_y = field.shape[2]
    cols_z = field.shape[3]
    padded_yz = wrap_pad(wrap_pad(field, 2), 3)
    laplace = 3.0 * lap_weights[0] * field
    for offset in range(1, 5):
        weight = lap_weights[offset]
        along_x = (
            padded_x[:, 4 + offset : 4 + offset + planes]
            + padded_x[:, 4 - offset : 4 - offset + planes]
        )
        along_y = (
            padded_yz[:, :, 4 + offset : 4 + offset + rows_y, 4 : 4 + cols_z]
            + padded_yz[:, :, 4 - offset : 4 - offset + rows_y, 4 : 4 + cols_z]
        )
        along_z = (
            padded_yz[:, :, 4 : 4 + rows_y, 4 + offset : 4 + offset + cols_z]
            + padded_yz[:, :, 4 : 4 + rows_y, 4 - offset : 4 - offset + cols_z]
        )
        laplace = laplace + weight * (along_x + along_y + along_z)
    return potential[None] * field - 0.5 * laplace


def operate_whole(field, potential):
    return operate(wrap_pad(field, 1), field, potential)


def filter_with(apply_op, start_field, potential):
    center = 0.5 * (upper_edge + lower_edge)
    half_width = 0.5 * (upper_edge - lower_edge)
    prev_field = start_field
    this_field = (apply_op(start_field, potential) - center * start_field) / half_width
    for degree in range(2):
        next_field = (
            2.0 * (apply_op(this_field, potential) - center * this_field) / half_width - prev_field
        )
        prev_field, this_field = (this_field, next_field)
    return this_field


def per_device(orbitals, potential):
    whole_orbs = lax.all_to_all(orbitals, "grid", split_axis=0, concat_axis=1, tiled=True)
    whole_potential = lax.all_gather(potential, "grid", axis=0, tiled=True)
    whole_filtered = filter_with(operate_whole, whole_orbs, whole_potential)
    this_field = lax.all_to_all(whole_filtered, "grid", split_axis=1, concat_axis=0, tiled=True)
    local_orbs = orbitals.shape[0]
    field_shape = this_field.shape
    flat_field = this_field.reshape(local_orbs, -1)
    total_cells = float(flat_field.shape[1] * lax.axis_size("grid"))
    contract = (((1,), (1,)), ((), ()))
    highest = lax.Precision.HIGHEST
    gathered = lax.all_gather(flat_field, "orb", axis=0, tiled=True)
    partial_rows = lax.dot_general(flat_field, gathered, contract, precision=highest)
    summed_rows = lax.psum(partial_rows, "grid")
    margin = lax.all_gather(summed_rows, "orb", axis=0, tiled=True) / total_cells
    factor = jnp.linalg.cholesky(margin)
    identity = jnp.eye(margin.shape[0], dtype=jnp.float32)
    inverse = jax.scipy.linalg.solve_triangular(factor, identity, lower=True)
    first_row = lax.axis_index("orb") * local_orbs
    own_rows = lax.dynamic_slice_in_dim(inverse, first_row, local_orbs, 0)
    rotated = jnp.dot(own_rows, gathered, precision=highest)
    return rotated.reshape(field_shape)


def solution(mesh):
    in_specs = (P("orb", "grid", None, None), P("grid", None, None))
    out_specs = P("orb", "grid", None, None)
    return jax.shard_map(
        per_device, mesh=mesh, in_specs=in_specs, out_specs=out_specs, check_vma=False
    )
```

profile of v0, /device:TPU:0, one launch (start us, length us, event | category | flops | bytes accessed | tf_op | source)
XLA Modules:
  0.0 627.1 jit_solution(10983866723867046044)
XLA Ops:
  6.5 5.3 all-to-all-start
  11.9 30.0 %all_gather.9 = f32[32,8,128]{2,1,0:T(8,128)S(1)} all-gather(f32[4,8,128]{2,1,0:T(8,128)S(1)} %copy-done.9), channel_id=1, replica_groups=mesh['grid'=8,'orb'=4] {'grid'}, dimensions={0}, use_global_device_ids=true | all-gather | bytes 147456 | tf_op jit(solution)/shard_map/all_gather | solution.py:61
  42.6 1.3 copy-done.6
  43.9 1.8 copy.12
  46.1 0.8 fusion.167
  46.9 0.8 pad_maximum_fusion.3
  47.7 1.6 fusion.162
  49.3 9.7 %pad_maximum_fusion = (f32[16,32,16,132]{3,2,1,0:T(8,128)}, f32[16,32,16,132]{3,2,1,0:T(8,128)}) fusion(f32[16,32,16,4]{3,2,1,0:T(8,128)S(1)} %get-tuple-element.35, f32[16,32,4,128]{3,2,1,0:T(4,128)S(1)} %get-tuple-element.48, f32[16,32,8,128]{3,2,1,0:T(8,128)S(1)} %bitcast.68, f32[16,32,4,128]{3,2,1,0:T(4,128)S(1)} %get-tuple-element.47, ...), kind=kLoop, calls=%fused_computation.2 | loop fusion | flops 6488064 | bytes 13107200 | tf_op jit(solution)/shard_map/concatenate | solution.py:15
  59.0 30.3 %broadcast_multiply_fusion = (f32[16,32,8,128]{3,2,1,0:T(8,128)}, f32[16,32,8,128]{3,2,1,0:T(8,128)}) fusion(f32[16,32,8,128]{3,2,1,0:T(8,128)S(1)} %bitcast.69, f32[16,32,16,132]{3,2,1,0:T(8,128)} %get-tuple-element.34, f32[16,32,16,132]{3,2,1,0:T(8,128)} %get-tuple-element.33, f32[16,32,4,128]{3,2,1,0:T(4,128)S(1)} %get-tuple-element.47, ...), kind=kLoop, calls=%fused_computation.246 | loop fusion | flops 26738688 | bytes 25821184 | tf_op jit(solution)/shard_map/div | solution.py:50
  89.3 2.7 fusion.165
  92.2 0.8 fusion.166
  93.0 0.8 pad_maximum_fusion.4
  93.8 1.6 fusion.161
  95.4 9.6 %pad_maximum_fusion.1 = (f32[16,32,16,132]{3,2,1,0:T(8,128)}, f32[16,32,16,132]{3,2,1,0:T(8,128)}) fusion(f32[16,32,16,4]{3,2,1,0:T(8,128)S(1)} %get-tuple-element.31, f32[16,32,4,128]{3,2,1,0:T(4,128)S(1)} %get-tuple-element.41, f32[16,32,8,128]{3,2,1,0:T(8,128)S(1)} %copy-done.1, f32[16,32,4,128]{3,2,1,0:T(4,128)S(1)} %get-tuple-element.42, ...), kind=kLoop, calls=%fused_computation.4 | loop fusion | flops 6488064 | bytes 13107200 | tf_op jit(solution)/shard_map/concatenate | solution.py:15
  104.9 43.1 %fusion.38 = f32[16,32,8,128]{3,2,1,0:T(8,128)} fusion(f32[16,32,8,128]{3,2,1,0:T(8,128)S(1)} %bitcast.70, f32[16,32,8,128]{3,2,1,0:T(8,128)} %get-tuple-element.21, f32[16,4,8,128]{3,2,1,0:T(8,128)} %get-tuple-element.44, f32[16,4,8,128]{3,2,1,0:T(8,128)S(1)} %get-tuple-element.43, f32[16,32,4,128]{3,2,1,0:T(4,128)} %copy-done.5, ...), kind=kLoop, calls=%fused_computation.121 | loop fusion | flops 27262976 | bytes 27918336 | tf_op jit(solution)/shard_map/sub | solution.py:53
  148.0 2.7 fusion.163
  150.9 0.8 fusion.164
  151.7 0.8 pad_maximum_fusion.5
  152.5 1.6 fusion.160
  154.1 9.6 %pad_maximum_fusion.2 = (f32[16,32,16,132]{3,2,1,0:T(8,128)}, f32[16,32,16,132]{3,2,1,0:T(8,128)}) fusion(f32[16,32,16,4]{3,2,1,0:T(8,128)S(1)} %get-tuple-element.27, f32[16,32,4,128]{3,2,1,0:T(4,128)S(1)} %get-tuple-element.37, f32[16,32,8,128]{3,2,1,0:T(8,128)S(1)} %copy-done, f32[16,32,4,128]{3,2,1,0:T(4,128)S(1)} %get-tuple-element.38, ...), kind=kLoop, calls=%fused_computation.6 | loop fusion | flops 6488064 | bytes 13107200 | tf_op jit(solution)/shard_map/concatenate | solution.py:15
  163.7 30.3 %fusion.11 = f32[16,32,8,128]{3,2,1,0:T(8,128)} fusion(f32[16,32,8,128]{3,2,1,0:T(8,128)S(1)} %copy-done, f32[16,4,8,128]{3,2,1,0:T(8,128)} %get-tuple-element.40, f32[16,4,8,128]{3,2,1,0:T(8,128)S(1)} %get-tuple-element.39, f32[16,32,4,128]{3,2,1,0:T(4,128)} %copy-done.3, f32[16,32,4,128]{3,2,1,0:T(4,128)S(1)} %get-tuple-element.37, ...), kind=kLoop, calls=%fused_computation.94 | loop fusion | flops 27787264 | bytes 25821184 | tf_op jit(solution)/shard_map/sub | solution.py:53
  194.0 1.8 copy.13
  195.8 29.1 %all_to_all.33 = f32[16,32,8,128]{3,2,0,1:T(8,128)S(1)} all-to-all(f32[16,32,8,128]{3,2,0,1:T(8,128)S(1)} %copy.13), channel_id=1, replica_groups=mesh['grid'=8,'orb'=4] {'grid'}, dimensions={1} | all-to-all | bytes 4194304 | tf_op jit(solution)/shard_map/all_to_all | solution.py:63
  225.2 1.5 reshape.47
  226.8 149.1 %all-gather.3.cloned.1.call-done = f32[512,4096]{1,0:T(8,128)} async-done(((f32[128,4096]{1,0:T(8,128)}), f32[512,4096]{1,0:T(8,128)}) %all-gather.3.cloned.1.call-update) | async-done | bytes 8388624 | tf_op jit(solution)/shard_map/all_gather | solution.py:70
  375.9 9.7 %fusion.169 = f32[128,512]{0,1:T(8,128)} fusion(f32[128,4096]{1,0:T(8,128)S(1)} %copy-done.2, f32[512,4096]{1,0:T(8,128)} %all-gather.3.cloned.1.call-done), kind=kOutput, calls=%fused_computation.317 | convolution fusion | flops 3221225472 | bytes 10747904 | tf_op jit(solution)/shard_map/dot_general | solution.py:71
  385.9 52.0 %all-reduce.3.cloned.1.call-done = f32[128,512]{0,1:T(8,128)} async-done(((f32[128,512]{0,1:T(8,128)}), f32[128,512]{0,1:T(8,128)}) %all-reduce.3.cloned.1.call-update) | async-done | bytes 262160 | tf_op jit(solution)/shard_map/psum | solution.py:72
  438.0 1.1 fusion.130
  439.1 29.7 %all-gather.5.cloned.1.call-done = f32[512,512]{0,1:T(8,128)} async-done(((f32[128,512]{0,1:T(8,128)}), f32[512,512]{0,1:T(8,128)}) %all-gather.5.cloned.1.call-update) | async-done | bytes 1048592 | tf_op jit(solution)/shard_map/all_gather | solution.py:73
  468.8 1.4 broadcast_multiply_fusion.1
  470.8 11.7 %cholesky.104 = f32[128,128]{1,0:T(8,128)S(1)} custom-call(f32[128,128]{1,0:T(8,128)S(1)} %cholesky.266), custom_call_target="Cholesky" | custom-call | tf_op jit(solution)/shard_map/jit(cholesky)/cholesky | solution.py:74
  482.7 9.8 %custom-call.31 = f32[1,128,128]{1,2,0:T(8,128)S(1)} custom-call(f32[1,128,128]{2,1,0:T(8,128)S(1)} %get-tuple-element.58), custom_call_target="InvertDiagBlocksLowerTriangular" | custom-call | tf_op jit(solution)/shard_map/jit(cholesky)/cholesky | solution.py:74
  493.2 11.7 %cholesky.217 = f32[128,128]{1,0:T(8,128)S(1)} custom-call(f32[128,128]{1,0:T(8,128)S(1)} %cholesky.270), custom_call_target="Cholesky" | custom-call | tf_op jit(solution)/shard_map/jit(cholesky)/cholesky | solution.py:74
  504.9 10.0 %custom-call.32 = f32[1,128,128]{1,2,0:T(8,128)S(1)} custom-call(f32[1,128,128]{2,1,0:T(8,128)S(1)} %get-tuple-element.55), custom_call_target="InvertDiagBlocksLowerTriangular" | custom-call | tf_op jit(solution)/shard_map/jit(cholesky)/cholesky | solution.py:74
  515.6 12.3 %cholesky.238 = f32[128,128]{1,0:T(8,128)} custom-call(f32[128,128]{1,0:T(8,128)S(1)} %cholesky.275), custom_call_target="Cholesky" | custom-call | tf_op jit(solution)/shard_map/jit(cholesky)/cholesky | solution.py:74
  527.9 1.6 select_reduce_fusion.1
  530.1 11.3 %custom-call.33 = f32[1,128,128]{1,2,0:T(8,128)} custom-call(f32[1,128,128]{2,1,0:T(8,128)} %get-tuple-element.52), custom_call_target="InvertDiagBlocksLowerTriangular" | custom-call | tf_op jit(solution)/shard_map/jit(cholesky)/cholesky | solution.py:74
  541.4 1.0 convolution_dynamic-update-slice_fusion.1
  542.8 11.9 %cholesky.255 = f32[128,128]{1,0:T(8,128)S(1)} custom-call(f32[128,128]{1,0:T(8,128)S(1)} %convolution_subtract_fusion.5), custom_call_target="Cholesky" | custom-call | tf_op jit(solution)/shard_map/jit(cholesky)/cholesky | solution.py:74
  555.4 0.7 compare_reduce_fusion.2
  558.6 9.7 %while.1 = (s32[]{:T(128)}, f32[512,512]{1,0:T(8,128)S(1)}, s32[4,2]{0,1:T(2,128)S(1)}, f32[4,128,128]{2,1,0:T(8,128)}, s32[]{:T(128)}) while((s32[]{:T(128)}, f32[512,512]{1,0:T(8,128)S(1)}, s32[4,2]{0,1:T(2,128)S(1)}, f32[4,128,128]{2,1,0:T(8,128)}, s32[]{:T(128)}) %tuple.40), condition=%wide.while_cond, body=%wide.while_body.sunk | while | flops 2 | bytes 132705 | solution.py:76
  559.2 1.8 bitcast_dynamic-update-slice_fusion.2
  561.6 1.8 bitcast_dynamic-update-slice_fusion.2
  564.1 1.8 bitcast_dynamic-update-slice_fusion.2
  566.5 1.8 bitcast_dynamic-update-slice_fusion.2
  568.3 40.1 %custom-call.34 = f32[4,128,128]{1,2,0:T(8,128)S(1)} custom-call(f32[4,128,128]{2,1,0:T(8,128)} %get-tuple-element.12), custom_call_target="InvertDiagBlocksLowerTriangular" | custom-call | tf_op jit(solution)/shard_map/jit(_solve_triangular)/triangular_solve | solution.py:76
  611.5 7.1 %convolution_bitcast_fusion = f32[16,8,32,128]{3,1,2,0:T(8,128)S(1)} fusion(f32[512,4096]{1,0:T(8,128)} %all-gather.3.cloned.1.call-done, s32[]{:T(128)S(6)} %select_n.8, f32[128,512]{1,0:T(8,128)S(1)} %fusion.136, f32[128,512]{1,0:T(8,128)S(1)} %fusion.148, f32[128,512]{1,0:T(8,128)S(1)} %fusion.146, f32[128,512]{1,0:T(8,128)S(1)} %fusion.145), kind=kOutput, calls=%fused_computation.229 | convolution fusion | flops 3221422080 | bytes 11534340 | tf_op jit(solution)/shard_map/dot_general | solution.py:79
  618.6 1.7 copy.18
  (65 shorter events, 11.1 us)
Async XLA Ops:
  6.5 5.4 copy-start.9
  6.5 36.1 %all-to-all-start = ((f32[128,4,8,128]{3,2,1,0:T(8,128)}), f32[128,4,8,128]{3,2,1,0:T(8,128)S(1)}, u32[]{:S(2)}, u32[]{:S(2)}) async-start(f32[128,4,8,128]{3,2,1,0:T(8,128)} %param.2), calls=%async_computation | async-start | bytes 4194304 | tf_op jit(solution)/shard_map/all_to_all | solution.py:60
  11.9 364.1 %all-gather.3.cloned.1.call-start = ((), (), s32[]{:S(2)}) async-start(), calls=%async_computation.2 | async-start | bytes 10485760 | tf_op jit(solution)/shard_map/all_gather | solution.py:70
  42.6 1.3 copy-start.6
  46.1 3.2 copy-start.4
  89.3 2.9 copy-start.1
  92.2 3.2 copy-start.5
  148.0 2.9 copy-start
  150.8 3.2 copy-start.3
  226.8 149.2 %copy-start.2 = (f32[128,4096]{1,0:T(8,128)S(1)}, f32[128,4096]{1,0:T(8,128)}, u32[]{:S(2)}) copy-start(f32[128,4096]{1,0:T(8,128)} %reshape.47) | copy-start | bytes 6291460
  226.8 211.1 %all-reduce.3.cloned.1.call-start = ((), (), s32[]{:S(2)}) async-start(), calls=%async_computation.3 | async-start | bytes 524288 | tf_op jit(solution)/shard_map/psum | solution.py:72
  385.7 83.2 %all-gather.5.cloned.1.call-start = ((), (), s32[]{:S(2)}) async-start(), calls=%async_computation.4 | async-start | bytes 1310720 | tf_op jit(solution)/shard_map/all_gather | solution.py:73
  468.8 1.8 copy-start.7
  527.9 80.8 %copy-start.8 = (f32[512,512]{1,0:T(8,128)S(1)}, f32[512,512]{1,0:T(8,128)}, u32[]{:S(2)}) copy-start(f32[512,512]{1,0:T(8,128)} %fusion.130) | copy-start | bytes 3145732
Sparse Core Ops, SparseCore 0:
  226.9 148.9 all-gather.2
  385.8 52.0 all-reduce.2
  439.5 29.3 all-gather.4
where the time goes:
time: 631 us; the launch traced here: 627 us
  other arithmetic  261 us (41%)
  waiting for transfers between devices  231 us (37%)
  blocking collectives  59.1 us (9%)
  local copies, waits for them, and re-layouts  31.9 us (5%)
  matrix products  22.5 us (4%)
  between operations  16.2 us (3%)
    all_gather x1, waiting for transfers between devices, per_device(): gathered = lax.all_gather(flat_field, 'orb', axis=0, tiled=True)  149 us
    another operation x14, other arithmetic, per_device(): factor = jnp.linalg.cholesky(margin)  82.3 us
    sub x2, other arithmetic, filter_with(): 2.0 * (apply_op(this_field, potential) - center * this_field) / half_width  73.4 us
    psum x1, waiting for transfers between devices, per_device(): summed_rows = lax.psum(partial_rows, 'grid')  52 us
    another operation x3, other arithmetic, per_device(): inverse = jax.scipy.linalg.solve_triangular(factor, identity, lower=True)  40.3 us
    concatenate x6, other arithmetic, wrap_pad(): return jnp.concatenate([head, field, tail], axis=axis_num)  31.3 us
    div x1, other arithmetic, filter_with(): (apply_op(start_field, potential) - center * start_field) / half_width  30.3 us
    all_gather x1, blocking collectives, per_device(): whole_potential = lax.all_gather(potential, 'grid', axis=0, tiled=True)  30 us
  transfers between devices with their start and end apart: 4, of which 3 were waited for; matrix products, arithmetic and copies ran while one was open for 0% of the time, Pallas kernels for 0%

commit v1 on v0

v1 whole, which is shorter than its diff:
```python
import jax
import jax.numpy as jnp
from jax import lax
from jax.experimental import pallas as pl
from jax.experimental.pallas import tpu as pltpu
from jax.sharding import PartitionSpec as P

lap_weights = (-205.0 / 72.0, 8.0 / 5.0, -1.0 / 5.0, 8.0 / 315.0, -1.0 / 560.0)
lower_edge = 3.0
upper_edge = 11.0
center = 0.5 * (upper_edge + lower_edge)
half_width = 0.5 * (upper_edge - lower_edge)
highest = lax.Precision.HIGHEST
bf16 = jnp.bfloat16
f32 = jnp.float32


def y_sums(v):
    rows = v.shape[1]
    if rows == 8:
        one = pltpu.roll(v, 1, 1) + pltpu.roll(v, 7, 1)
        half = pltpu.roll(v, 4, 1)
        return one, pltpu.roll(v + half, 2, 1), pltpu.roll(one, 4, 1), half + half
    return tuple(pltpu.roll(v, m, 1) + pltpu.roll(v, rows - m, 1) for m in range(1, 5))


def filter_kernel(x_ref, pot_ref, out_ref, first, second, third):
    slabs, orbs, planes, rows, cols = x_ref.shape
    nx = slabs * planes

    def load(x, carry):
        first[x] = x_ref[x // planes, :, x % planes]
        return carry

    lax.fori_loop(0, nx, load, 0)

    def apply(src, x, factor):
        v = src[x]
        diag = (pot_ref[x] - (1.5 * lap_weights[0] + center)) * (factor / half_width)
        acc = diag[None] * v
        ys = y_sums(v)
        for m in range(1, 5):
            up = lax.rem(x + m, nx)
            down = lax.rem(x + (nx - m), nx)
            along_z = pltpu.roll(v, m, 2) + pltpu.roll(v, cols - m, 2)
            total = (src[up] + src[down]) + (along_z + ys[m - 1])
            acc = acc + (-0.5 * lap_weights[m] * factor / half_width) * total
        return acc

    def level1(x, carry):
        second[x] = apply(first, x, 1.0)
        return carry

    def level2(x, carry):
        third[x] = apply(second, x, 2.0) - first[x]
        return carry

    def level3(x, carry):
        value = apply(third, x, 2.0) - second[x]
        out_ref[x % planes, x // planes] = jnp.swapaxes(value, 0, 1)
        return carry

    lax.fori_loop(0, nx, level1, 0)
    lax.fori_loop(0, nx, level2, 0)
    lax.fori_loop(0, nx, level3, 0)


def filter_orbitals(x, pot):
    slabs, orbs, planes, rows, cols = x.shape
    buf = pltpu.VMEM((slabs * planes, orbs, rows, cols), f32)
    return pl.pallas_call(
        filter_kernel,
        out_shape=jax.ShapeDtypeStruct((planes, slabs, rows, orbs, cols), f32),
        in_specs=[pl.BlockSpec(memory_space=pltpu.VMEM)] * 2,
        out_specs=pl.BlockSpec(memory_space=pltpu.VMEM),
        scratch_shapes=[buf, buf, buf],
        compiler_params=pltpu.CompilerParams(vmem_limit_bytes=56 << 20),
        name="filter",
    )(x, pot)


def split(value):
    high = value.astype(bf16)
    return high, (value - high.astype(f32)).astype(bf16)


def block_list(count):
    return [(i, j) for i in range(count) for j in range(i, count)]


def margin_kernel(f_ref, out_ref, high, low):
    parts, rows, orbs, cols = f_ref.shape
    norb = parts * orbs
    for r in range(rows):
        h, l = split(f_ref[:, r].reshape(norb, cols))
        high[:, r * cols : (r + 1) * cols] = h
        low[:, r * cols : (r + 1) * cols] = l
    size = out_ref.shape[-1]
    contract = (((1,), (1,)), ((), ()))
    at = 0
    for i in range(norb // size):
        mine = pl.ds(i * size, size)
        rest = pl.ds(i * size, norb - i * size)
        h, l = high[mine, :], low[mine, :]
        hr, lr = high[rest, :], low[rest, :]
        total = lax.dot_general(h, lr, contract, preferred_element_type=f32)
        total = total + lax.dot_general(l, hr, contract, preferred_element_type=f32)
        total = total + lax.dot_general(h, hr, contract, preferred_element_type=f32)
        for j in range(norb // size - i):
            out_ref[at] = total[:, j * size : (j + 1) * size]
            at += 1


def margin_blocks(f, size):
    parts, rows, orbs, cols = f.shape
    norb = parts * orbs
    count = norb // size
    return pl.pallas_call(
        margin_kernel,
        out_shape=jax.ShapeDtypeStruct((count * (count + 1) // 2, size, size), f32),
        in_specs=[pl.BlockSpec(memory_space=pltpu.VMEM)],
        out_specs=pl.BlockSpec(memory_space=pltpu.VMEM),
        scratch_shapes=[pltpu.VMEM((norb, rows * cols), bf16)] * 2,
        compiler_params=pltpu.CompilerParams(vmem_limit_bytes=56 << 20),
        name="margin",
    )(f)


def dot(a, b, contract=(1, 0)):
    dims = (((contract[0],), (contract[1],)), ((), ()))
    return lax.dot_general(a, b, dims, precision=highest, preferred_element_type=f32)


def inverse_kernel(m_ref, v_ref, work, wd, wi):
    size = m_ref.shape[-1]
    blocks = {}
    count = 0
    while count * (count + 1) // 2 < m_ref.shape[0]:
        count += 1
    for at, pair in enumerate(block_list(count)):
        blocks[pair] = at
    work[...] = m_ref[...]
    row = lax.broadcasted_iota(jnp.int32, (8, size), 0)
    lane = lax.broadcasted_iota(jnp.int32, (8, size), 1)

    def spread(value, k):
        return jnp.broadcast_to(value[k : k + 1, :], value.shape)

    def panel(s, carry):
        base = pl.multiple_of(s * 8, 8)
        pd = wd[pl.ds(base, 8), :]
        pi = wi[pl.ds(base, 8), :]
        rolled = pltpu.roll(pd, lax.rem(size - base, size), 1)
        cols = [jnp.broadcast_to(rolled[:, j : j + 1], (8, size)) for j in range(8)]
        scale = jnp.zeros((8, size), f32)
        for j in range(8):
            pivot = spread(cols[j], j)
            root = lax.rsqrt(pivot)
            root = root * (1.5 - 0.5 * pivot * root * root)
            scale = jnp.where(row == j, root, scale)
            if j < 7:
                factor = jnp.where(row > j, cols[j], 0.0) * (root * root)
                for k in range(j + 1, 8):
                    cols[k] = cols[k] - factor * spread(cols[j], k)
                pd = pd - factor * spread(pd, j)
                pi = pi - factor * spread(pi, j)
        pd = pd * scale
        pi = pi * scale
        wi[pl.ds(base, 8), :] = pi
        left = jnp.where(lane >= base + 8, pd, 0.0)
        wd[...] = wd[...] - dot(left, pd, (0, 0))
        wi[...] = wi[...] - dot(left, pi, (0, 0))
        return carry

    for k in range(count):
        wd[...] = work[blocks[k, k]]
        r0 = lax.broadcasted_iota(jnp.int32, (size, size), 0)
        c0 = lax.broadcasted_iota(jnp.int32, (size, size), 1)
        wi[...] = jnp.where(r0 == c0, 1.0, 0.0)
        lax.fori_loop(0, size // 8, panel, 0)
        inv = wi[...]
        for j in range(k):
            v_ref[blocks[j, k]] = dot(inv, v_ref[blocks[j, k]])
        v_ref[blocks[k, k]] = inv
        right = {j: dot(inv, work[blocks[k, j]]) for j in range(k + 1, count)}
        for i in range(k + 1, count):
            for j in range(i, count):
                work[blocks[i, j]] = work[blocks[i, j]] - dot(right[i], right[j], (0, 0))
            for j in range(k + 1):
                term = dot(right[i], v_ref[blocks[j, k]], (0, 0))
                if j == k:
                    v_ref[blocks[j, i]] = -term
                else:
                    v_ref[blocks[j, i]] = v_ref[blocks[j, i]] - term


def inverse_blocks(m):
    size = m.shape[-1]
    return pl.pallas_call(
        inverse_kernel,
        out_shape=jax.ShapeDtypeStruct(m.shape, f32),
        in_specs=[pl.BlockSpec(memory_space=pltpu.VMEM)],
        out_specs=pl.BlockSpec(memory_space=pltpu.VMEM),
        scratch_shapes=[
            pltpu.VMEM(m.shape, f32),
            pltpu.VMEM((size, size), f32),
            pltpu.VMEM((size, size), f32),
        ],
        compiler_params=pltpu.CompilerParams(vmem_limit_bytes=56 << 20),
        name="inverse",
    )(m)


def rotate_kernel(v_ref, f_ref, out_ref):
    parts, rows, orbs, cols = f_ref.shape
    owners, local = out_ref.shape[0], out_ref.shape[1]
    size = v_ref.shape[-1]
    norb = parts * orbs
    count = norb // size
    vs = {}
    for at, (j, i) in enumerate(block_list(count)):
        vs[i, j] = split(v_ref[at])
    for r in range(0, rows, 2):
        wide = min(2, rows - r)
        pieces = [f_ref[:, r + e].reshape(norb, cols) for e in range(wide)]
        high, low = split(jnp.concatenate(pieces, axis=1) if wide > 1 else pieces[0])
        for i in range(count):
            vh = jnp.concatenate([vs[i, j][0] for j in range(i + 1)], axis=1)
            vl = jnp.concatenate([vs[i, j][1] for j in range(i + 1)], axis=1)
            upto = (i + 1) * size
            total = jnp.dot(vh, low[:upto], preferred_element_type=f32)
            total = total + jnp.dot(vl, high[:upto], preferred_element_type=f32)
            total = total + jnp.dot(vh, high[:upto], preferred_element_type=f32)
            step = min(size, local)
            for q in range(size // step):
                row0 = i * size + q * step
                own, off = row0 // local, row0 % local
                for e in range(wide):
                    out_ref[own, pl.ds(off, step), r + e, :] = total[
                        q * step : (q + 1) * step, e * cols : (e + 1) * cols
                    ]


def rotate(v, f, owners):
    parts, rows, orbs, cols = f.shape
    norb = parts * orbs
    return pl.pallas_call(
        rotate_kernel,
        out_shape=jax.ShapeDtypeStruct((owners, norb // owners, rows, cols), f32),
        in_specs=[pl.BlockSpec(memory_space=pltpu.VMEM)] * 2,
        out_specs=pl.BlockSpec(memory_space=pltpu.VMEM),
        compiler_params=pltpu.CompilerParams(vmem_limit_bytes=56 << 20),
        name="rotate",
    )(v, f)


def per_device(orbitals, potential):
    local, planes, rows, cols = orbitals.shape
    slabs = lax.axis_size("grid")
    owners = lax.axis_size("orb")
    norb = local * owners
    orbs = local // slabs
    everyone = ("orb", "grid")

    whole = lax.all_to_all(orbitals, "grid", split_axis=0, concat_axis=0, tiled=True)
    pot = lax.all_gather(potential, "grid", axis=0, tiled=True)
    filtered = filter_orbitals(whole.reshape(slabs, orbs, planes, rows, cols), pot)

    if planes >= owners:
        each = planes // owners
        part_rows = each * rows
        filtered = filtered.reshape(owners, each, slabs, rows, orbs, cols)
        filtered = jnp.swapaxes(filtered, 1, 2)
    else:
        each = owners // planes
        part_rows = rows // each
        filtered = filtered.reshape(planes, slabs, each, part_rows, orbs, cols)
        filtered = jnp.swapaxes(filtered, 1, 2)
    filtered = filtered.reshape(owners * slabs, part_rows, orbs, cols)
    cells = lax.all_to_all(filtered, everyone, split_axis=0, concat_axis=0, tiled=True)

    size = 128
    partial = margin_blocks(cells, size)
    blocks = partial.shape[0]
    devices = owners * slabs
    total_cells = float(planes * slabs * rows * cols)
    mixed = lax.all_to_all(
        partial.reshape(devices, blocks * size // devices, size), everyone, split_axis=0, concat_axis=0, tiled=True
    )
    own = jnp.sum(mixed, axis=0) / total_cells
    margin = lax.all_gather(own, everyone, axis=0, tiled=True).reshape(blocks, size, size)
    inverse = inverse_blocks(margin)
    rotated = rotate(inverse, cells, owners)
    back = lax.all_to_all(rotated, "orb", split_axis=0, concat_axis=0, tiled=True)
    return jnp.swapaxes(back, 0, 1).reshape(local, planes, rows, cols)


def solution(mesh):
    in_specs = (P("orb", "grid", None, None), P("grid", None, None))
    out_specs = P("orb", "grid", None, None)
    return jax.shard_map(per_device, mesh=mesh, in_specs=in_specs, out_specs=out_specs, check_vma=False)
```

time: 631 us -> 286 us (0.45)
  other arithmetic: 261 us -> 0.06 us
  waiting for transfers between devices: 231 us -> 0.01 us
  blocking collectives: 59.1 us -> 203 us
  Pallas kernels: 0 us -> 74.8 us
  local copies, waits for them, and re-layouts: 31.9 us -> 2.93 us
  matrix products: 22.5 us -> 0 us
  between operations: 16.2 us -> 0.01 us
    all_gather x2 -> x0, waiting for transfers between devices: 179 us -> none  [the longest x1 149 us: per_device(): gathered = lax.all_gather(flat_field, 'orb', axis=0, tiled=True)]
    another operation x17 -> x0, other arithmetic: 123 us -> none  [the longest x14 82.3 us: per_device(): factor = jnp.linalg.cholesky(margin)]
    all_to_all x1 -> x3, blocking collectives: 29.1 us -> 128 us  [the longest x1 53.7 us: per_device(): lax.all_to_all(filtered, everyone, split_axis=0, concat_axis=0, tiled=True)]
    pallas_call x0 -> x4, Pallas kernels: none -> 74.8 us  [the longest x1 40.7 us: inverse_blocks(): pl.pallas_call(inverse_kernel, out_shape=jax.ShapeDtypeStruct(m.shape, f3...]
    sub x2 -> x0, other arithmetic: 73.4 us -> none  [filter_with(): 2.0 * (apply_op(this_field, potential) - center * this_field) / half_width]
    psum x1 -> x0, waiting for transfers between devices: 52 us -> none  [per_device(): summed_rows = lax.psum(partial_rows, 'grid')]
    all_gather x1 -> x2, blocking collectives: 30 us -> 74.6 us  [the longest x1 43.8 us: per_device(): lax.all_gather(own, everyone, axis=0, tiled=True)]
    div x3 -> x1, other arithmetic: 31.9 us -> 0.01 us  [per_device(): own = jnp.sum(mixed, axis=0) / total_cells]
  transfers between devices with their start and end apart: 4 -> 1, of which waited for: 3 -> 0; matrix products, arithmetic and copies ran while one was open for 0% -> 0% of each run, Pallas kernels for 0% -> 0%
where the time goes in v1:
time: 286 us
  blocking collectives  203 us (71%)
  Pallas kernels  74.8 us (26%)
  starting transfers between devices  5.33 us (2%)
  local copies, waits for them, and re-layouts  2.93 us (1%)
    all_to_all x1, blocking collectives, per_device(): lax.all_to_all(filtered, everyone, split_axis=0, concat_axis=0, tiled=True)  53.7 us
    all_to_all x1, blocking collectives, per_device(): lax.all_to_all(rotated, 'orb', split_axis=0, concat_axis=0, tiled=True)  52.6 us
    all_gather x1, blocking collectives, per_device(): lax.all_gather(own, everyone, axis=0, tiled=True)  43.8 us
    pallas_call x1, Pallas kernels, inverse_blocks(): pl.pallas_call(inverse_kernel, out_shape=jax.ShapeDtypeStruct(m.shape, f3...  40.7 us
    all_gather x1, blocking collectives, per_device(): pot = lax.all_gather(potential, 'grid', axis=0, tiled=True)  30.8 us
    pallas_call x1, Pallas kernels, filter_orbitals(): pl.pallas_call(filter_kernel, out_shape=jax.ShapeDtypeStruct((planes, sla...  24 us
    all_to_all x1, blocking collectives, per_device(): lax.all_to_all(partial.reshape(devices, blocks * size // devices, size),...  21.7 us
  transfers between devices with their start and end apart: 1, of which 0 were waited for; matrix products, arithmetic and copies ran while one was open for 0% of the time, Pallas kernels for 0%

profile of v1, /device:TPU:0, one launch (start us, length us, event | category | flops | bytes accessed | tf_op | source)
XLA Modules:
  0.0 285.7 jit_solution(13474663804379631403)
XLA Ops:
  0.0 0.0 copy-start.1
  0.0 5.3 %all-to-all-start = ((f32[128,4,8,128]{3,2,1,0:T(8,128)}), f32[128,4,8,128]{3,2,1,0:T(8,128)S(1)}, u32[]{:S(2)}, u32[]{:S(2)}) async-start(f32[128,4,8,128]{3,2,1,0:T(8,128)} %param.2), calls=%async_computation | async-start | bytes 4194304 | tf_op jit(solution)/shard_map/all_to_all | solution.py:265
  5.3 0.0 copy-done.1
  5.3 30.8 %all_gather.6.pot_ref = f32[32,8,128]{2,1,0:T(8,128)} all-gather(f32[4,8,128]{2,1,0:T(8,128)S(1)} %copy-done.1), channel_id=1, replica_groups=mesh['grid'=8,'orb'=4] {'grid'}, dimensions={0}, use_global_device_ids=true | all-gather | bytes 147456 | tf_op jit(solution)/shard_map/all_gather | solution.py:266
  36.2 0.0 all-to-all-done
  36.2 0.0 copy-start
  36.2 1.3 copy-done
  37.5 24.0 %filter.1 = f32[4,8,8,16,128]{4,3,2,1,0:T(8,128)} custom-call(f32[8,16,4,8,128]{4,3,2,1,0:T(8,128)} %bitcast.5, f32[32,8,128]{2,1,0:T(8,128)} %all_gather.6.pot_ref), custom_call_target="tpu_custom_call" | custom-call | tf_op jit(solution)/shard_map/filter/pallas_call | solution.py:71
  61.5 53.7 %all_to_all.20.f_ref = f32[32,8,16,128]{3,2,1,0:T(8,128)} all-to-all(f32[32,8,16,128]{3,2,1,0:T(8,128)} %bitcast.6), channel_id=1, replica_groups=mesh['grid'=8,'orb'=4] {'orb','grid'}, dimensions={0} | all-to-all | bytes 4194304 | tf_op jit(solution)/shard_map/all_to_all | solution.py:280
  115.2 5.0 %margin.1 = f32[10,128,128]{2,1,0:T(8,128)} custom-call(f32[32,8,16,128]{3,2,1,0:T(8,128)} %all_to_all.20.f_ref), custom_call_target="tpu_custom_call" | custom-call | tf_op jit(solution)/shard_map/margin/pallas_call | solution.py:118
  120.1 21.7 %all_to_all.21 = f32[32,40,128]{2,1,0:T(8,128)S(1)} all-to-all(f32[32,40,128]{2,1,0:T(8,128)} %bitcast.9), channel_id=1, replica_groups=mesh['grid'=8,'orb'=4] {'orb','grid'}, dimensions={0} | all-to-all | bytes 1310720 | tf_op jit(solution)/shard_map/all_to_all | solution.py:287
  141.8 0.1 reduce_sum.9
  141.9 43.8 %all_gather.7 = f32[1280,128]{1,0:T(8,128)} all-gather(f32[40,128]{1,0:T(8,128)S(1)} %broadcast_multiply_fusion), channel_id=1, replica_groups=mesh['grid'=8,'orb'=4] {'orb','grid'}, dimensions={0}, use_global_device_ids=true | all-gather | bytes 675840 | tf_op jit(solution)/shard_map/all_gather | solution.py:291
  185.7 40.7 %inverse.1.v_ref = f32[10,128,128]{2,1,0:T(8,128)} custom-call(f32[10,128,128]{2,1,0:T(8,128)} %bitcast.8), custom_call_target="tpu_custom_call" | custom-call | tf_op jit(solution)/shard_map/inverse/pallas_call | solution.py:199
  226.4 5.1 %rotate.1 = f32[4,128,8,128]{3,2,1,0:T(8,128)} custom-call(f32[10,128,128]{2,1,0:T(8,128)} %inverse.1.v_ref, f32[32,8,16,128]{3,2,1,0:T(8,128)} %all_to_all.20.f_ref), custom_call_target="tpu_custom_call" | custom-call | tf_op jit(solution)/shard_map/rotate/pallas_call | solution.py:247
  231.5 52.6 %all_to_all.22 = f32[4,128,8,128]{3,2,1,0:T(8,128)S(1)} all-to-all(f32[4,128,8,128]{3,2,1,0:T(8,128)} %rotate.1), channel_id=1, replica_groups=mesh['grid'=8,'orb'=4] {'orb'}, dimensions={0} | all-to-all | bytes 4194304 | tf_op jit(solution)/shard_map/all_to_all | solution.py:294
  284.1 1.6 copy.4
  (1 shorter events, 0.0 us)
Async XLA Ops:
  0.0 5.3 %copy-start.1 = (f32[4,8,128]{2,1,0:T(8,128)S(1)}, f32[4,8,128]{2,1,0:T(8,128)}, u32[]{:S(2)}) copy-start(f32[4,8,128]{2,1,0:T(8,128)} %param.3) | copy-start | bytes 49156
  0.0 36.2 %all-to-all-start = ((f32[128,4,8,128]{3,2,1,0:T(8,128)}), f32[128,4,8,128]{3,2,1,0:T(8,128)S(1)}, u32[]{:S(2)}, u32[]{:S(2)}) async-start(f32[128,4,8,128]{3,2,1,0:T(8,128)} %param.2), calls=%async_computation | async-start | bytes 4194304 | tf_op jit(solution)/shard_map/all_to_all | solution.py:265
  36.2 1.3 copy-start
